TPU v7x, 32 devices: a whole 2x2x4 slice. The times are simulated.
32 devices in a mesh: groups: 2 (over x), out: 16 (over z, y, core).
Axes of the slice: x: 2, y: 2, z: 4, core: 2. Of those that a mesh axis runs over, the one named last changes fastest.
Arguments:
- tokens: bfloat16 [256, 8192], P('groups', 'out'), parts along dimension 0, may hold values from -60 to 60, as said below
- grad_hidden: bfloat16 [256, 16384], P('groups', 'out'), parts along dimension 0, may hold values from -6 to 6
- w_gate: bfloat16 [8192, 16384], P(None, 'out'), may hold values from -0.0625 to 0.0625
- w_up: bfloat16 [8192, 16384], P(None, 'out'), may hold values from -0.0625 to 0.0625
- a_factors: bfloat16 [8192, 128], replicated, may hold values from -0.0625 to 0.0625
- b_factors: bfloat16 [2, 64, 16384], P(None, None, 'out'), may hold values from -0.75 to 0.75
- magnitudes: float32 [2, 16384], P(None, 'out'), may hold values from 1 to 2
Outputs:
- hidden: bfloat16 [256, 16384], P('groups', 'out'), parts along dimension 0
- grad_tokens: bfloat16 [256, 8192], P('groups', 'out'), parts along dimension 0
- step_a: float32 [16384, 128], P(('groups', 'out')), parts along dimension 0
- step_b: float32 [4, 64, 16384], P('groups', None, 'out'), parts along dimension 0
- step_m: float32 [4, 16384], P('groups', 'out'), parts along dimension 0
There are 2 independent parts, one for each index of `groups`. A program takes and returns all parts, laid end to end along the dimension named above; an argument that names none is the same for every part. Nothing has to cross between parts.
Inputs may be any that keep to these rules, and one draw needn't show every extreme that they name: `tokens`: activations with feature scales that differ between features.
All inputs are finite; a program needn't handle non-finite values.
Results may differ from a plain program's by a relative error of at most 0.0073.
Values may be sent and summed in bfloat16 or wider, within the bound.
A program may use at most 128 MiB of HBM per device.

v0:
```python
import jax
import jax.numpy as jnp
from jax import lax
from jax.sharding import PartitionSpec as P

D = 8192
FW = 16384
R = 64


def inner_product(left_side, right_side, precision=None):
    return lax.dot_general(
        left_side,
        right_side,
        (((0,), (0,)), ((), ())),
        precision=precision,
        preferred_element_type=jnp.float32,
    )


def outer_contract(left_side, right_side, precision=None):
    return lax.dot_general(
        left_side,
        right_side,
        (((1,), (1,)), ((), ())),
        precision=precision,
        preferred_element_type=jnp.float32,
    )


def split_parts(values):
    upper = values.astype(jnp.bfloat16)
    lower = (values - upper.astype(jnp.float32)).astype(jnp.bfloat16)
    return (upper, lower)


def per_device(tokens, grad_hidden, w_gate, w_up, a_factors, b_factors, magnitudes):
    weights = (w_gate, w_up)
    rank = a_factors.shape[1] // 2
    count_tokens = tokens.shape[0]
    norms = []
    scales = []
    for which in range(2):
        weight = weights[which]
        left = a_factors[:, which * rank : (which + 1) * rank]
        right = b_factors[which]
        merged = weight.astype(jnp.float32) + jnp.dot(
            left, right, preferred_element_type=jnp.float32
        )
        squares = jnp.sum(merged * merged, axis=0)
        norm_col = jnp.sqrt(squares + 1e-06)
        norms.append(norm_col)
        scales.append(magnitudes[which] / norm_col)
    whole = lax.all_gather(tokens, "out", axis=1, tiled=True)
    base_gate = jnp.dot(whole, w_gate, preferred_element_type=jnp.float32)
    base_up = jnp.dot(whole, w_up, preferred_element_type=jnp.float32)
    low_wide = jnp.dot(whole, a_factors, preferred_element_type=jnp.float32)
    low = low_wide.astype(jnp.bfloat16)
    bases = []
    pres = []
    for which, raw in enumerate((base_gate, base_up)):
        base = raw + jnp.dot(
            low[:, which * rank : (which + 1) * rank],
            b_factors[which],
            preferred_element_type=jnp.float32,
        )
        bases.append(base)
        pres.append(base * scales[which][None, :])
    sigma = jax.nn.sigmoid(pres[0])
    hidden = (pres[0] * sigma * pres[1]).astype(jnp.bfloat16)
    cotangent = grad_hidden.astype(jnp.float32)
    dpres = (
        cotangent * pres[1] * sigma * (1.0 + pres[0] * (1.0 - sigma)),
        cotangent * pres[0] * sigma,
    )
    partial_sum = jnp.zeros((count_tokens, w_gate.shape[0]), jnp.float32)
    z_blocks = []
    grad_bs = []
    grad_ms = []
    for which in range(2):
        dscaled = (dpres[which] * scales[which][None, :]).astype(jnp.bfloat16)
        grad_ms.append(jnp.sum(dpres[which] * bases[which], axis=0) / norms[which])
        grad_bs.append(inner_product(low[:, which * rank : (which + 1) * rank], dscaled))
        z_blocks.append(outer_contract(dscaled, b_factors[which]))
        partial_sum = partial_sum + outer_contract(dscaled, weights[which])
    z_local = jnp.concatenate(z_blocks, axis=1)
    z_upper, z_lower = split_parts(z_local)
    partial_sum = (
        partial_sum + outer_contract(z_upper, a_factors) + outer_contract(z_lower, a_factors)
    )
    a_terms = inner_product(whole, z_upper) + inner_product(whole, z_lower)
    grad_a = lax.psum_scatter(a_terms, "out", scatter_dimension=0, tiled=True)
    summed_inputs = lax.psum_scatter(partial_sum, "out", scatter_dimension=1, tiled=True)
    grad_tokens = summed_inputs.astype(jnp.bfloat16)
    grad_b = jnp.stack(grad_bs)
    grad_m = jnp.stack(grad_ms)
    local_energy = jnp.sum(grad_a * grad_a) + jnp.sum(grad_b * grad_b) + jnp.sum(grad_m * grad_m)
    energy = lax.psum(local_energy, "out")
    count_all = 2 * D * R + 2 * R * FW + 2 * FW
    rms_value = jnp.sqrt(energy / count_all + 1e-06)
    return (hidden, grad_tokens, grad_a / rms_value, grad_b / rms_value, grad_m / rms_value)


def solution(mesh):
    in_specs = (
        P("groups", "out"),
        P("groups", "out"),
        P(None, "out"),
        P(None, "out"),
        P(),
        P(None, None, "out"),
        P(None, "out"),
    )
    out_specs = (
        P("groups", "out"),
        P("groups", "out"),
        P(("groups", "out"), None),
        P("groups", None, "out"),
        P("groups", "out"),
    )
    return jax.shard_map(
        per_device, mesh=mesh, in_specs=in_specs, out_specs=out_specs, check_vma=False
    )
```

profile of v0, /device:TPU:0, one launch (start us, length us, event | category | flops | bytes accessed | tf_op | source)
XLA Modules:
  0.0 230.4 jit_solution(6841040627441248489)
XLA Ops:
  8.0 8.9 %multiply_reduce_fusion.1 = f32[1024]{0:T(1024)S(1)} fusion(bf16[8192,1024]{1,0:T(8,128)(2,1)} %param.9, bf16[8192,128]{1,0:T(8,128)(2,1)} %param.11, bf16[2,64,1024]{2,1,0:T(8,128)(2,1)} %param.12), kind=kOutput, calls=%fused_computation.1 | convolution fusion | flops 1107295232 | bytes 19009536 | tf_op jit(solution)/shard_map/dot_general | solution.py:47
  16.9 2.9 %copy-done = bf16[8192,1024]{1,0:T(8,128)(2,1)S(1)} copy-done((bf16[8192,1024]{1,0:T(8,128)(2,1)S(1)}, bf16[8192,1024]{1,0:T(8,128)(2,1)}, u32[]{:S(2)}) %copy-start) | copy-done | bytes 16777240
  19.8 5.5 %multiply_reduce_fusion = f32[1024]{0:T(1024)S(1)} fusion(bf16[8192,1024]{1,0:T(8,128)(2,1)S(1)} %copy-done, bf16[8192,128]{1,0:T(8,128)(2,1)S(1)} %copy-done.2, bf16[2,64,1024]{2,1,0:T(8,128)(2,1)S(1)} %copy-done.3), kind=kOutput, calls=%fused_computation | convolution fusion | flops 1107295232 | bytes 19009536 | tf_op jit(solution)/shard_map/dot_general | solution.py:47
  25.4 28.7 %all-gather.2.cloned.1.call-done = bf16[128,8192]{1,0:T(8,128)(2,1)} async-done(((bf16[128,512]{1,0:T(8,128)(2,1)}), bf16[128,8192]{1,0:T(8,128)(2,1)}) %all-gather.2.cloned.1.call-update) | async-done | bytes 2097168 | tf_op jit(solution)/shard_map/all_gather | solution.py:54
  54.1 2.7 %convolution_convert_fusion = bf16[128,128]{0,1:T(8,128)(2,1)S(1)} fusion(bf16[128,8192]{1,0:T(8,128)(2,1)} %all-gather.2.cloned.1.call-done, bf16[8192,128]{1,0:T(8,128)(2,1)S(1)} %copy-done.2), kind=kOutput, calls=%fused_computation.13 | convolution fusion | flops 268451840 | bytes 4227072 | tf_op jit(solution)/shard_map/dot_general | solution.py:57
  56.8 8.9 %fusion.32 = f32[128,1024]{1,0:T(8,128)S(1)} fusion(bf16[128,8192]{1,0:T(8,128)(2,1)} %all-gather.2.cloned.1.call-done, bf16[8192,1024]{1,0:T(8,128)(2,1)} %param.10), kind=kOutput, calls=%fused_computation.62 | convolution fusion | flops 2147483648 | bytes 19398656 | tf_op jit(solution)/shard_map/dot_general | solution.py:56
  66.0 0.8 slice-done.3
  67.4 2.4 %fusion.31 = f32[128,1024]{1,0:T(8,128)S(1)} fusion(bf16[128,8192]{1,0:T(8,128)(2,1)S(1)} %copy-done.1, bf16[8192,1024]{1,0:T(8,128)(2,1)S(1)} %bitcast.47), kind=kOutput, calls=%fused_computation.61 | convolution fusion | flops 2147483648 | bytes 19398656 | tf_op jit(solution)/shard_map/dot_general | solution.py:55
  69.9 1.3 multiply_reduce_fusion.3
  71.6 0.7 fusion.26
  72.3 2.6 %fusion = f32[8192,128]{0,1:T(8,128)} fusion(f32[128,8192]{1,0:T(8,128)S(1)} %fusion.26, bf16[128,8192]{1,0:T(8,128)(2,1)S(1)} %copy-done.1, f32[128,64]{0,1:T(8,128)S(1)} %fusion.7, f32[128,64]{0,1:T(8,128)S(1)} %fusion.11), kind=kOutput, calls=%fused_computation.3 | convolution fusion | flops 269565952 | bytes 10551296 | tf_op jit(solution)/shard_map/dot_general | solution.py:12
  75.3 13.5 %fusion.33 = f32[128,8192]{1,0:T(8,128)} fusion(bf16[128,1024]{1,0:T(8,128)(2,1)S(1)} %get-tuple-element.12, bf16[8192,1024]{1,0:T(8,128)(2,1)} %param.9), kind=kOutput, calls=%fused_computation.63 | convolution fusion | flops 2147483648 | bytes 21233664 | tf_op jit(solution)/shard_map/dot_general | solution.py:22
  88.8 15.3 %convolution_add_fusion.3 = f32[128,8192]{1,0:T(8,128)} fusion(f32[128,8192]{1,0:T(8,128)} %fusion.33, bf16[128,1024]{1,0:T(8,128)(2,1)S(1)} %get-tuple-element.14, bf16[8192,1024]{1,0:T(8,128)(2,1)} %param.10), kind=kOutput, calls=%fused_computation.6 | convolution fusion | flops 2148532224 | bytes 25427968 | tf_op jit(solution)/shard_map/dot_general | solution.py:22
  104.1 3.0 %convolution_add_fusion.2 = f32[128,8192]{1,0:T(8,128)S(1)} fusion(f32[128,8192]{1,0:T(8,128)} %convolution_add_fusion.3, bf16[8192,128]{1,0:T(8,128)(2,1)S(1)} %copy-done.2, f32[128,64]{0,1:T(8,128)S(1)} %fusion.7, f32[128,64]{0,1:T(8,128)S(1)} %fusion.11), kind=kOutput, calls=%fused_computation.5 | convolution fusion | flops 269549568 | bytes 10551296 | tf_op jit(solution)/shard_map/dot_general | solution.py:22
  107.1 2.8 %convolution_add_fusion.1 = f32[128,8192]{1,0:T(8,128)} fusion(f32[128,8192]{1,0:T(8,128)S(1)} %convolution_add_fusion.2, bf16[8192,128]{1,0:T(8,128)(2,1)S(1)} %copy-done.2, f32[128,64]{0,1:T(8,128)S(1)} %fusion.7, f32[128,64]{0,1:T(8,128)S(1)} %fusion.11), kind=kOutput, calls=%fused_computation.4 | convolution fusion | flops 269565952 | bytes 10551296 | tf_op jit(solution)/shard_map/dot_general | solution.py:22
  110.9 0.7 multiply_reduce_fusion.4
  111.6 34.9 %reduce-scatter.5.cloned.1.call-done = f32[512,128]{0,1:T(8,128)} async-done(((f32[8192,128]{0,1:T(8,128)}), f32[512,128]{0,1:T(8,128)}) %reduce-scatter.5.cloned.1.call-update) | async-done | bytes 262160 | tf_op jit(solution)/shard_map/reduce_scatter | solution.py:92
  146.5 1.6 multiply_reduce_fusion.5
  150.1 30.5 %psum.7 = f32[]{:T(128)} all-reduce(f32[]{:T(128)S(6)} %add.92), channel_id=1, replica_groups=mesh['groups'=2,'out'=16] {'out'}, use_global_device_ids=true, to_apply=%region_9.0 | all-reduce | flops 1 | bytes 8 | tf_op jit(solution)/shard_map/psum | solution.py:98
  181.3 1.0 broadcast_divide_fusion
  182.3 0.8 copy.12
  183.8 0.9 fusion.6
  184.6 37.7 %reduce-scatter.3.cloned.1.call-done = f32[128,512]{1,0:T(8,128)} async-done(((f32[128,8192]{1,0:T(8,128)}), f32[128,512]{1,0:T(8,128)}) %reduce-scatter.3.cloned.1.call-update) | async-done | bytes 262160 | tf_op jit(solution)/shard_map/reduce_scatter | solution.py:93
  222.3 1.6 convert_element_type.43
  (37 shorter events, 3.9 us)
Async XLA Ops:
  7.2 46.9 %all-gather.2.cloned.1.call-start = ((), (), s32[]{:S(2)}) async-start(), calls=%async_computation.2 | async-start | bytes 2228224 | tf_op jit(solution)/shard_map/all_gather | solution.py:54
  7.9 9.0 %copy-start.2 = (bf16[8192,128]{1,0:T(8,128)(2,1)S(1)}, bf16[8192,128]{1,0:T(8,128)(2,1)}, u32[]{:S(2)}) copy-start(bf16[8192,128]{1,0:T(8,128)(2,1)} %param.11) | copy-start | bytes 6291460
  7.9 9.0 %copy-start.3 = (bf16[2,64,1024]{2,1,0:T(8,128)(2,1)S(1)}, bf16[2,64,1024]{2,1,0:T(8,128)(2,1)}, u32[]{:S(2)}) copy-start(bf16[2,64,1024]{2,1,0:T(8,128)(2,1)} %param.12) | copy-start | bytes 786436
  7.9 138.6 %reduce-scatter.5.cloned.1.call-start = ((), (), s32[]{:S(2)}) async-start(), calls=%async_computation.4 | async-start | bytes 4456448 | tf_op jit(solution)/shard_map/reduce_scatter | solution.py:92
  8.0 11.9 %copy-start = (bf16[8192,1024]{1,0:T(8,128)(2,1)S(1)}, bf16[8192,1024]{1,0:T(8,128)(2,1)}, u32[]{:S(2)}) copy-start(bf16[8192,1024]{1,0:T(8,128)(2,1)} %param.10) | copy-start | bytes 50331652
  19.8 5.6 %copy-start.4 = (f32[2,1024]{1,0:T(2,128)S(1)}, f32[2,1024]{1,0:T(2,128)}, u32[]{:S(2)}) copy-start(f32[2,1024]{1,0:T(2,128)} %param.13) | copy-start | bytes 24580
  54.1 11.9 %slice-start = ((s8[16777216]{0:T(1024)(128)(4,1)}), s8[4194304]{0:T(1024)(128)(4,1)S(1)}, s32[]{:S(2)}) async-start(s8[16777216]{0:T(1024)(128)(4,1)} %bitcast.46), calls=%async_computation.5 | async-start | bytes 8388608
  56.8 9.2 %slice-start.1 = ((s8[16777216]{0:T(1024)(128)(4,1)}), s8[4194304]{0:T(1024)(128)(4,1)S(1)}, s32[]{:S(2)}) async-start(s8[16777216]{0:T(1024)(128)(4,1)} %bitcast.46), calls=%async_computation.6 | async-start | bytes 8388608
  56.8 9.2 %slice-start.2 = ((s8[16777216]{0:T(1024)(128)(4,1)}), s8[4194304]{0:T(1024)(128)(4,1)S(1)}, s32[]{:S(2)}) async-start(s8[16777216]{0:T(1024)(128)(4,1)} %bitcast.46), calls=%async_computation.7 | async-start | bytes 8388608
  56.8 10.0 %slice-start.3 = ((s8[16777216]{0:T(1024)(128)(4,1)}), s8[4194304]{0:T(1024)(128)(4,1)S(1)}, s32[]{:S(2)}) async-start(s8[16777216]{0:T(1024)(128)(4,1)} %bitcast.46), calls=%async_computation.8 | async-start | bytes 8388608
  56.8 10.6 %copy-start.1 = (bf16[128,8192]{1,0:T(8,128)(2,1)S(1)}, bf16[128,8192]{1,0:T(8,128)(2,1)}, u32[]{:S(2)}) copy-start(bf16[128,8192]{1,0:T(8,128)(2,1)} %all-gather.2.cloned.1.call-done) | copy-start | bytes 6291460
  67.4 2.5 %copy-start.5 = (bf16[128,1024]{1,0:T(8,128)(2,1)S(1)}, bf16[128,1024]{1,0:T(8,128)(2,1)}, u32[]{:S(2)}) copy-start(bf16[128,1024]{1,0:T(8,128)(2,1)} %param.8) | copy-start | bytes 786436
  75.0 147.3 %reduce-scatter.3.cloned.1.call-start = ((), (), s32[]{:S(2)}) async-start(), calls=%async_computation.3 | async-start | bytes 4456448 | tf_op jit(solution)/shard_map/reduce_scatter | solution.py:93
Sparse Core Ops, SparseCore 0:
  10.2 43.8 all-gather.1
  75.1 71.3 reduce-scatter.4
  150.9 71.3 reduce-scatter.2
where the time goes:
time: 231 us; the launch traced here: 230 us
  waiting for transfers between devices  102 us (44%)
  matrix products  68.7 us (30%)
  blocking collectives  30.5 us (13%)
  between operations  16.6 us (7%)
  other arithmetic  7.07 us (3%)
  local copies, waits for them, and re-layouts  5.15 us (2%)
    reduce_scatter x1, waiting for transfers between devices, per_device(): lax.psum_scatter(partial_sum, 'out', scatter_dimension=1, tiled=True)  37.7 us
    dot_general x6, matrix products, outer_contract(): lax.dot_general(left_side, right_side, (((1,), (1,)), ((), ())), precisio...  35 us
    reduce_scatter x1, waiting for transfers between devices, per_device(): grad_a = lax.psum_scatter(a_terms, 'out', scatter_dimension=0, tiled=True)  34.9 us
    psum x1, blocking collectives, per_device(): energy = lax.psum(local_energy, 'out')  30.5 us
    all_gather x1, waiting for transfers between devices, per_device(): whole = lax.all_gather(tokens, 'out', axis=1, tiled=True)  28.7 us
    dot_general x2, matrix products, per_device(): jnp.dot(left, right, preferred_element_type=jnp.float32)  14.5 us
    dot_general x1, matrix products, per_device(): base_up = jnp.dot(whole, w_up, preferred_element_type=jnp.float32)  8.88 us
    unnamed x21, local copies, waits for them, and re-layouts  5.15 us
  transfers between devices with their start and end apart: 3, of which 3 were waited for; matrix products, arithmetic and copies ran while one was open for 24% of the time, Pallas kernels for 0%

commit v1 on v0

--- a/solution.py
+++ b/solution.py
@@ -6,6 +6,28 @@
 D = 8192
 FW = 16384
 R = 64
+
+
+def resolve_edges_up(sheet, k_dim):
+    b_now = list(sheet.shape[1:])
+    b_now[k_dim] *= sheet.shape[0]
+    return jnp.moveaxis(sheet, 0, k_dim).reshape(b_now)
+
+
+def tell_goods(unit, named_axis):
+    size_here = lax.axis_size(named_axis)
+    extra = unit[None]
+    for k0 in range(size_here.bit_length() - 1):
+        reply = 1 << k0
+        a_now = lax.ppermute(
+            extra,
+            axis_name=named_axis,
+            perm=list(map(lambda no: (no, no ^ reply), range(size_here))),
+        )
+        found_now = jnp.stack([extra, a_now])
+        big = lax.axis_index(named_axis) >> k0 & 1
+        extra = jnp.where(big == 0, found_now, found_now[::-1]).reshape(-1, *unit.shape)
+    return extra
 
 
 def inner_product(left_side, right_side, precision=None):
@@ -51,7 +73,11 @@
         norm_col = jnp.sqrt(squares + 1e-06)
         norms.append(norm_col)
         scales.append(magnitudes[which] / norm_col)
-    whole = lax.all_gather(tokens, "out", axis=1, tiled=True)
+
+    def plane_update(arr, inp, along_dim):
+        return resolve_edges_up(tell_goods(arr, inp), along_dim)
+
+    whole = plane_update(tokens, "out", 1)
     base_gate = jnp.dot(whole, w_gate, preferred_element_type=jnp.float32)
     base_up = jnp.dot(whole, w_up, preferred_element_type=jnp.float32)
     low_wide = jnp.dot(whole, a_factors, preferred_element_type=jnp.float32)

time: 231 us -> 260 us (1.13)
  waiting for transfers between devices: 102 us -> 121 us
  starting transfers between devices: 0.34 us -> 8.11 us
  other arithmetic: 7.07 us -> 11.2 us
  local copies, waits for them, and re-layouts: 5.15 us -> 2.46 us
    ppermute x0 -> x4, waiting for transfers between devices: none -> 46.8 us  [tell_goods(): lax.ppermute(extra, axis_name=named_axis, perm=list(map(lambda no: (no, n...]
    all_gather x1 -> x0, waiting for transfers between devices: 28.7 us -> none  [per_device(): whole = lax.all_gather(tokens, 'out', axis=1, tiled=True)]
    ppermute x0 -> x4, starting transfers between devices: none -> 7.81 us  [tell_goods(): lax.ppermute(extra, axis_name=named_axis, perm=list(map(lambda no: (no, n...]
    unnamed x21 -> x18, local copies, waits for them, and re-layouts: 5.15 us -> 1.13 us
    dot_general x2, matrix products: 14.5 us -> 17.6 us  [per_device(): jnp.dot(left, right, preferred_element_type=jnp.float32)]
  transfers between devices with their start and end apart: 3 -> 6, of which waited for: 3 -> 6; matrix products, arithmetic and copies ran while one was open for 24% -> 23% of each run, Pallas kernels for 0% -> 0%
where the time goes in v1:
time: 260 us
  waiting for transfers between devices  121 us (47%)
  matrix products  69.9 us (27%)
  blocking collectives  30.7 us (12%)
  between operations  17 us (7%)
  other arithmetic  11.2 us (4%)
  starting transfers between devices  8.11 us (3%)
    ppermute x4, waiting for transfers between devices, tell_goods(): lax.ppermute(extra, axis_name=named_axis, perm=list(map(lambda no: (no, n...  46.8 us
    reduce_scatter x1, waiting for transfers between devices, per_device(): lax.psum_scatter(partial_sum, 'out', scatter_dimension=1, tiled=True)  37.9 us
    reduce_scatter x1, waiting for transfers between devices, per_device(): grad_a = lax.psum_scatter(a_terms, 'out', scatter_dimension=0, tiled=True)  36.1 us
    dot_general x6, matrix products, outer_contract(): lax.dot_general(left_side, right_side, (((1,), (1,)), ((), ())), precisio...  35.5 us
    psum x1, blocking collectives, per_device(): energy = lax.psum(local_energy, 'out')  30.7 us
    dot_general x2, matrix products, per_device(): jnp.dot(left, right, preferred_element_type=jnp.float32)  17.6 us
    dot_general x1, matrix products, per_device(): base_up = jnp.dot(whole, w_up, preferred_element_type=jnp.float32)  8.4 us
    ppermute x4, starting transfers between devices, tell_goods(): lax.ppermute(extra, axis_name=named_axis, perm=list(map(lambda no: (no, n...  7.81 us
  transfers between devices with their start and end apart: 6, of which 6 were waited for; matrix products, arithmetic and copies ran while one was open for 23% of the time, Pallas kernels for 0%

profile of v1, /device:TPU:0, one launch (start us, length us, event | category | flops | bytes accessed | tf_op | source)
XLA Modules:
  0.0 260.0 jit_solution(12982847017695518344)
XLA Ops:
  7.7 1.2 collective-permute-done
  9.9 2.9 %collective-permute-start.1 = (bf16[2,128,512]{2,1,0:T(8,128)(2,1)S(1)}, bf16[2,128,512]{2,1,0:T(8,128)(2,1)S(1)}, u32[]{:S(2)}, u32[]{:S(2)}) collective-permute-start(bf16[2,128,512]{2,1,0:T(8,128)(2,1)S(1)} %get-tuple-element.11), channel_id=1, source_target_pairs={{0,2},{1,3},{2,0},{3,1},{4,6},{5,7},{6,4},{7,5},{8,10},{9,11},{10,... | collective-permute-start | bytes 786440 | tf_op jit(solution)/shard_map/ppermute | solution.py:22
  12.9 6.6 %collective-permute-done.1 = bf16[2,128,512]{2,1,0:T(8,128)(2,1)S(1)} collective-permute-done((bf16[2,128,512]{2,1,0:T(8,128)(2,1)S(1)}, bf16[2,128,512]{2,1,0:T(8,128)(2,1)S(1)}, u32[]{:S(2)}, u32[]{:S(2)}) %collective-permute-start.1) | collective-permute-done | bytes 262176 | tf_op jit(solution)/shard_map/ppermute | solution.py:22
  19.6 1.9 collective-permute-start.2
  21.5 8.8 %multiply_reduce_fusion.1 = f32[1024]{0:T(1024)S(1)} fusion(bf16[8192,1024]{1,0:T(8,128)(2,1)} %param.9, bf16[8192,128]{1,0:T(8,128)(2,1)} %param.11, bf16[2,64,1024]{2,1,0:T(8,128)(2,1)} %param.12), kind=kOutput, calls=%fused_computation.1 | convolution fusion | flops 1107295232 | bytes 19009536 | tf_op jit(solution)/shard_map/dot_general | solution.py:69
  30.3 2.8 %collective-permute-done.2 = bf16[4,128,512]{2,1,0:T(8,128)(2,1)S(1)} collective-permute-done((bf16[4,128,512]{2,1,0:T(8,128)(2,1)S(1)}, bf16[4,128,512]{2,1,0:T(8,128)(2,1)S(1)}, u32[]{:S(2)}, u32[]{:S(2)}) %collective-permute-start.2) | collective-permute-done | bytes 524320 | tf_op jit(solution)/shard_map/ppermute | solution.py:22
  33.5 1.3 copy.12
  34.8 2.5 collective-permute-start.3
  37.3 8.8 %multiply_reduce_fusion = f32[1024]{0:T(1024)S(1)} fusion(bf16[8192,1024]{1,0:T(8,128)(2,1)} %param.10, bf16[8192,128]{1,0:T(8,128)(2,1)S(1)} %copy-done, bf16[2,64,1024]{2,1,0:T(8,128)(2,1)S(1)} %copy-done.2), kind=kOutput, calls=%fused_computation | convolution fusion | flops 1107295232 | bytes 19009536 | tf_op jit(solution)/shard_map/dot_general | solution.py:69
  46.2 36.1 %collective-permute-done.3 = bf16[8,128,512]{1,2,0:T(8,128)(2,1)} collective-permute-done((bf16[8,128,512]{1,2,0:T(8,128)(2,1)}, bf16[8,128,512]{1,2,0:T(8,128)(2,1)}, u32[]{:S(2)}, u32[]{:S(2)}) %collective-permute-start.3) | collective-permute-done | bytes 1048608 | tf_op jit(solution)/shard_map/ppermute | solution.py:22
  82.3 1.4 pad_maximum_fusion
  85.6 8.4 %convolution_add_fusion.4 = f32[128,1024]{1,0:T(8,128)S(1)} fusion(f32[128,1024]{1,0:T(8,128)S(1)} %fusion.11, bf16[128,8192]{0,1:T(8,128)(2,1)S(1)} %bitcast.64, bf16[8192,1024]{1,0:T(8,128)(2,1)} %param.10), kind=kOutput, calls=%fused_computation.11 | convolution fusion | flops 2147614720 | bytes 19922944 | tf_op jit(solution)/shard_map/dot_general | solution.py:82
  95.1 3.5 %multiply_reduce_fusion.3 = (f32[1024]{0:T(1024)S(1)}, f32[1024]{0:T(1024)S(1)}, bf16[128,1024]{1,0:T(8,128)(2,1)S(1)}, bf16[128,1024]{1,0:T(8,128)(2,1)}, bf16[128,1024]{1,0:T(8,128)(2,1)S(1)}) fusion(f32[1024]{0:T(1024)S(1)} %bitcast.83, f32[128,1024]{1,0:T(8,128)S(1)} %convolution_add_fusion.4, f32[1024]{0:T(1024)S(1)} %bitcast.84, ...), kind=kOutput, calls=%fused_computation.26 | convolution fusion | flops 2150889472 | bytes 20987904 | tf_op jit(solution)/shard_map/dot_general | solution.py:81
  99.8 2.6 %convolution_add_fusion = f32[8192,128]{1,0:T(8,128)} fusion(f32[8192,128]{1,0:T(8,128)S(1)} %fusion.29, bf16[128,8192]{0,1:T(8,128)(2,1)S(1)} %bitcast.67, f32[128,64]{0,1:T(8,128)S(1)} %fusion.8, f32[128,64]{0,1:T(8,128)S(1)} %fusion.13), kind=kOutput, calls=%fused_computation.2 | convolution fusion | flops 269565952 | bytes 10551296 | tf_op jit(solution)/shard_map/dot_general | solution.py:34
  102.7 13.3 %fusion.34 = f32[128,8192]{1,0:T(8,128)} fusion(bf16[128,1024]{1,0:T(8,128)(2,1)S(1)} %get-tuple-element.7, bf16[8192,1024]{1,0:T(8,128)(2,1)} %param.9), kind=kOutput, calls=%fused_computation.72 | convolution fusion | flops 2147483648 | bytes 21233664 | tf_op jit(solution)/shard_map/dot_general | solution.py:44
  116.0 15.5 %convolution_add_fusion.3 = f32[128,8192]{1,0:T(8,128)} fusion(f32[128,8192]{1,0:T(8,128)} %fusion.34, bf16[128,1024]{1,0:T(8,128)(2,1)S(1)} %get-tuple-element.9, bf16[8192,1024]{1,0:T(8,128)(2,1)} %param.10), kind=kOutput, calls=%fused_computation.5 | convolution fusion | flops 2148532224 | bytes 25427968 | tf_op jit(solution)/shard_map/dot_general | solution.py:44
  131.5 3.5 %convolution_add_fusion.2 = f32[128,8192]{1,0:T(8,128)S(1)} fusion(f32[128,8192]{1,0:T(8,128)} %convolution_add_fusion.3, bf16[8192,128]{1,0:T(8,128)(2,1)S(1)} %copy-done, f32[128,64]{0,1:T(8,128)S(1)} %fusion.8, f32[128,64]{0,1:T(8,128)S(1)} %fusion.13), kind=kOutput, calls=%fused_computation.4 | convolution fusion | flops 269549568 | bytes 10551296 | tf_op jit(solution)/shard_map/dot_general | solution.py:44
  135.0 2.8 %convolution_add_fusion.1 = f32[128,8192]{1,0:T(8,128)} fusion(f32[128,8192]{1,0:T(8,128)S(1)} %convolution_add_fusion.2, bf16[8192,128]{1,0:T(8,128)(2,1)S(1)} %copy-done, f32[128,64]{0,1:T(8,128)S(1)} %fusion.8, f32[128,64]{0,1:T(8,128)S(1)} %fusion.13), kind=kOutput, calls=%fused_computation.3 | convolution fusion | flops 269565952 | bytes 10551296 | tf_op jit(solution)/shard_map/dot_general | solution.py:44
  139.5 36.1 %reduce-scatter.5.cloned.1.call-done = f32[512,128]{1,0:T(8,128)} async-done(((f32[8192,128]{1,0:T(8,128)}), f32[512,128]{1,0:T(8,128)}) %reduce-scatter.5.cloned.1.call-update) | async-done | bytes 262160 | tf_op jit(solution)/shard_map/reduce_scatter | solution.py:118
  175.6 1.6 multiply_reduce_fusion.5
  179.2 30.7 %psum.7 = f32[]{:T(128)} all-reduce(f32[]{:T(128)S(6)} %add.88), channel_id=1, replica_groups=mesh['groups'=2,'out'=16] {'out'}, use_global_device_ids=true, to_apply=%region_9.10 | all-reduce | flops 1 | bytes 8 | tf_op jit(solution)/shard_map/psum | solution.py:124
  212.0 1.7 broadcast_divide_fusion
  213.7 37.9 %reduce-scatter.3.cloned.1.call-done = f32[128,512]{1,0:T(8,128)} async-done(((f32[128,8192]{1,0:T(8,128)}), f32[128,512]{1,0:T(8,128)}) %reduce-scatter.3.cloned.1.call-update) | async-done | bytes 262160 | tf_op jit(solution)/shard_map/reduce_scatter | solution.py:119
  251.6 1.6 convert_element_type.43
  (48 shorter events, 9.5 us)
Async XLA Ops:
  7.2 168.5 %reduce-scatter.5.cloned.1.call-start = ((), (), s32[]{:S(2)}) async-start(), calls=%async_computation.3 | async-start | bytes 4456448 | tf_op jit(solution)/shard_map/reduce_scatter | solution.py:118
  7.2 1.7 collective-permute-start
  9.9 9.6 %collective-permute-start.1 = (bf16[2,128,512]{2,1,0:T(8,128)(2,1)S(1)}, bf16[2,128,512]{2,1,0:T(8,128)(2,1)S(1)}, u32[]{:S(2)}, u32[]{:S(2)}) collective-permute-start(bf16[2,128,512]{2,1,0:T(8,128)(2,1)S(1)} %get-tuple-element.11), channel_id=1, source_target_pairs={{0,2},{1,3},{2,0},{3,1},{4,6},{5,7},{6,4},{7,5},{8,10},{9,11},{10,... | collective-permute-start | bytes 786440 | tf_op jit(solution)/shard_map/ppermute | solution.py:22
  19.6 13.5 %collective-permute-start.2 = (bf16[4,128,512]{2,1,0:T(8,128)(2,1)S(1)}, bf16[4,128,512]{2,1,0:T(8,128)(2,1)S(1)}, u32[]{:S(2)}, u32[]{:S(2)}) collective-permute-start(bf16[4,128,512]{2,1,0:T(8,128)(2,1)S(1)} %bitcast.70), channel_id=1, source_target_pairs={{0,4},{1,5},{2,6},{3,7},{4,0},{5,1},{6,2},{7,3},{8,12},{9,13},{10,... | collective-permute-start | bytes 1572872 | tf_op jit(solution)/shard_map/ppermute | solution.py:22
  30.3 7.0 %copy-start = (bf16[8192,128]{1,0:T(8,128)(2,1)S(1)}, bf16[8192,128]{1,0:T(8,128)(2,1)}, u32[]{:S(2)}) copy-start(bf16[8192,128]{1,0:T(8,128)(2,1)} %param.11) | copy-start | bytes 6291460
  30.3 7.0 %copy-start.2 = (bf16[2,64,1024]{2,1,0:T(8,128)(2,1)S(1)}, bf16[2,64,1024]{2,1,0:T(8,128)(2,1)}, u32[]{:S(2)}) copy-start(bf16[2,64,1024]{2,1,0:T(8,128)(2,1)} %param.12) | copy-start | bytes 786436
  34.8 11.4 %copy-start.4 = (f32[2,1024]{1,0:T(2,128)S(1)}, f32[2,1024]{1,0:T(2,128)}, u32[]{:S(2)}) copy-start(f32[2,1024]{1,0:T(2,128)} %param.13) | copy-start | bytes 24580
  34.8 47.5 %copy-start.1 = (bf16[2,4,128,512]{2,3,1,0:T(8,128)(2,1)S(1)}, bf16[2,4,128,512]{2,3,1,0:T(8,128)(2,1)}, u32[]{:S(2)}) copy-start(bf16[2,4,128,512]{2,3,1,0:T(8,128)(2,1)} %copy.12) | copy-start | bytes 3145732
  34.8 47.5 %collective-permute-start.3 = (bf16[8,128,512]{1,2,0:T(8,128)(2,1)}, bf16[8,128,512]{1,2,0:T(8,128)(2,1)}, u32[]{:S(2)}, u32[]{:S(2)}) collective-permute-start(bf16[8,128,512]{1,2,0:T(8,128)(2,1)} %bitcast.68), channel_id=1, source_target_pairs={{0,8},{1,9},{2,10},{3,11},{4,12},{5,13},{6,14},{7,15},{8,0},{9,1},... | collective-permute-start | bytes 3145736 | tf_op jit(solution)/shard_map/ppermute | solution.py:22
  84.3 9.8 %slice-start = ((s8[16777216]{0:T(1024)(128)(4,1)}), s8[4194304]{0:T(1024)(128)(4,1)S(1)}, s32[]{:S(2)}) async-start(s8[16777216]{0:T(1024)(128)(4,1)} %bitcast.61), calls=%async_computation.4 | async-start | bytes 8388608
  85.6 8.5 %slice-start.1 = ((s8[16777216]{0:T(1024)(128)(4,1)}), s8[4194304]{0:T(1024)(128)(4,1)S(1)}, s32[]{:S(2)}) async-start(s8[16777216]{0:T(1024)(128)(4,1)} %bitcast.61), calls=%async_computation.5 | async-start | bytes 8388608
  85.6 8.5 %slice-start.2 = ((s8[16777216]{0:T(1024)(128)(4,1)}), s8[4194304]{0:T(1024)(128)(4,1)S(1)}, s32[]{:S(2)}) async-start(s8[16777216]{0:T(1024)(128)(4,1)} %bitcast.61), calls=%async_computation.6 | async-start | bytes 8388608
  85.6 9.5 %slice-start.3 = ((s8[16777216]{0:T(1024)(128)(4,1)}), s8[4194304]{0:T(1024)(128)(4,1)S(1)}, s32[]{:S(2)}) async-start(s8[16777216]{0:T(1024)(128)(4,1)} %bitcast.61), calls=%async_computation.7 | async-start | bytes 8388608
  85.6 9.5 %copy-start.3 = (bf16[128,1024]{1,0:T(8,128)(2,1)S(1)}, bf16[128,1024]{1,0:T(8,128)(2,1)}, u32[]{:S(2)}) copy-start(bf16[128,1024]{1,0:T(8,128)(2,1)} %param.8) | copy-start | bytes 786436
  102.4 149.1 %reduce-scatter.3.cloned.1.call-start = ((), (), s32[]{:S(2)}) async-start(), calls=%async_computation.2 | async-start | bytes 4456448 | tf_op jit(solution)/shard_map/reduce_scatter | solution.py:119
Sparse Core Ops, SparseCore 0:
  102.5 73.0 reduce-scatter.4
  180.0 71.5 reduce-scatter.2
